TPU v7x, 512 devices: a whole 4x8x8 slice. The times are simulated.
512 devices in a mesh: crop: 4 (over x_lo, core), row: 128 (over y, x_hi, z).
Axes of the slice: x: 4 (x_hi: 2, x_lo: 2; x = x_hi * 2 + x_lo), y: 8, z: 8, core: 2. Of those that a mesh axis runs over, the one named last changes fastest.
Arguments:
- pair: bfloat16 [1024, 256, 128], P(('crop', 'row')), parts along dimension 0, may hold values from -6 to 6
- out_grad: bfloat16 [1024, 256, 128], P('crop', 'row'), parts along dimension 0, may hold values from -6 to 6
- w_qkvg: bfloat16 [128, 512], replicated, may hold values from -0.5 to 0.5
- w_out: bfloat16 [128, 128], replicated, may hold values from -0.5 to 0.5
- w_bias: bfloat16 [128, 4], replicated, may hold values from -32 to 32
- gain: float32 [128], replicated, may hold values from 0.1 to 1.9
Outputs:
- d_pair: bfloat16 [1024, 256, 128], P(('crop', 'row')), parts along dimension 0
- d_qkvg: float32 [512, 512], P('crop'), parts along dimension 0
- d_wout: float32 [512, 128], P('crop'), parts along dimension 0
- d_wbias: float32 [512, 4], P('crop'), parts along dimension 0
- d_gain: float32 [512], P('crop'), parts along dimension 0
There are 4 independent parts, one for each index of `crop`. A program takes and returns all parts, laid end to end along the dimension named above; an argument that names none is the same for every part. Nothing has to cross between parts.
All inputs are finite; a program needn't handle non-finite values.
Results may differ from a plain program's by a relative error of at most 0.014.
The roundings to bfloat16 on the way count: a program that leaves them out, or rounds other values in their place, can miss the bound.
Values may be sent and summed in bfloat16 or wider, within the bound.
No kernel may reach another device: no remote copies, remote signals or barrier semaphores. Data moves between devices by JAX's collectives and lax.ppermute only.
A program may use at most 64 MiB of HBM per device.

v0:
```python
import jax
import jax.numpy as jnp
from jax import lax
from jax.experimental import pallas as pl
from jax.experimental.pallas import tpu as pltpu
from jax.sharding import Mesh
from jax.sharding import PartitionSpec as P

DH = 32
H = 4
C = 128
N = 256
DEV = 128
W = 64
SCALE = DH ** (-0.5)
ROW = ("row_0", "row_1", "row_2")
CROP_ROW = ("crop", "row_0", "row_1", "row_2")
EPSILON = 1e-05
LOG2E = 1.4426950408889634
F32 = jnp.float32
BF16 = jnp.bfloat16


def dot(a, b, ca=1, cb=0):
    return lax.dot_general(a, b, (((ca,), (cb,)), ((), ())), preferred_element_type=F32)


def normalize(pair, gain):
    values = pair.astype(F32)
    center = jnp.mean(values, axis=-1, keepdims=True)
    spread = jnp.mean(jnp.square(values - center), axis=-1, keepdims=True)
    inv_std = lax.rsqrt(spread + EPSILON)
    normed = (values - center) * inv_std
    return ((normed * gain).astype(BF16), normed, inv_std)


def doubled(plane, m):
    own = plane.reshape(8, 2, 8, C)[:, m : m + 1]
    return jnp.concatenate([own, own], axis=1).reshape(128, C)


def member(rows, m):
    return rows.reshape(8, 2, 8, -1)[:, m].reshape(64, -1)


def pack_kernel(pair_ref, gain_ref, wbias_ref, out_ref, cells, packed):
    cells[...] = pair_ref[...].reshape(2 * N, C).astype(F32)
    bias = []
    for plane in range(4):
        r, c = plane // 2, plane % 2
        xn, _, _ = normalize(cells[pl.ds(r * N + c, 128, stride=2), :], gain_ref[...])
        bias.append(dot(wbias_ref[...], xn, 1, 1).astype(BF16).astype(F32))
        xn = xn.astype(F32)
        for m in range(2):
            packed[pl.ds(4 * m + plane, 128, stride=8), :] = doubled(xn, m)
    heads = [
        jnp.concatenate(
            [bias[plane][h : h + 1] for h in (2 * m, 2 * m + 1) for plane in range(4)], axis=0
        )
        for m in range(2)
    ]
    rows = jnp.concatenate([jnp.broadcast_to(x[None], (8, 8, C)) for x in heads], axis=0)
    rows = jnp.concatenate([rows] * 8, axis=0)
    out_ref[...] = jnp.concatenate([rows, packed[...].reshape(DEV, 8, C)], axis=1).astype(BF16)


def pack(pair, gain, w_bias):
    return pl.pallas_call(
        pack_kernel,
        out_shape=jax.ShapeDtypeStruct((DEV, 16, C), BF16),
        in_specs=vmem(3),
        out_specs=vmem(1)[0],
        scratch_shapes=[pltpu.VMEM((2 * N, C), F32), pltpu.VMEM((8 * DEV, C), F32)],
    )(pair, gain.reshape(1, C), w_bias.T)


def attention_kernel(cols_ref, grad_ref, w_ref, wt_ref, wout_ref, out_ref):
    def prepare(t):
        at = 8 + 4 * (t // 2) + t % 2
        tokens = jnp.concatenate([cols_ref[at], cols_ref[at + 2]], axis=0)
        grads = grad_ref[t]
        proj = dot(tokens, w_ref[:, : 3 * W]).astype(BF16)
        proj_t = dot(wt_ref[...], tokens, 1, 1)
        gate_t = jax.nn.sigmoid(proj_t[3 * W :])
        d_mixed_t = dot(wout_ref[...], grads, 1, 1)
        d_att_t = (d_mixed_t * gate_t).astype(BF16)
        return dict(
            tokens=tokens,
            grads=grads,
            q=proj[:, :W],
            k=proj[:, W : 2 * W],
            v=proj[:, 2 * W :],
            q_t=proj_t[:W].astype(BF16),
            k_t=proj_t[W : 2 * W].astype(BF16),
            v_t=proj_t[2 * W : 3 * W].astype(BF16),
            gate_t=gate_t,
            d_mixed_t=d_mixed_t,
            d_att_t=d_att_t,
            d_att=d_att_t.T,
            att_h=[],
            dq_h=[],
            d_k=None,
            d_v=None,
        )

    lane = lax.broadcasted_iota(jnp.int32, (N, W), 1) // DH
    zero = jnp.zeros((N, W), BF16)

    def raw(col, h):
        rows = slice(h * DH, (h + 1) * DH)
        s = dot(col["k"][:, rows], col["q_t"][rows])
        d_probs = dot(col["v"][:, rows], col["d_att_t"][rows])
        return s, d_probs

    def head(col, h, bias, s, d_probs):
        own = lane == h
        rows = slice(h * DH, (h + 1) * DH)
        s = s * (SCALE * LOG2E) + bias
        e = jnp.exp2(s - jnp.max(s, axis=0, keepdims=True))
        probs = e * (1.0 / jnp.sum(e, axis=0, keepdims=True))
        probs_b = probs.astype(BF16)
        att_h = dot(col["v_t"][rows], probs_b)
        delta = jnp.sum(col["d_att_t"][rows].astype(F32) * att_h, axis=0, keepdims=True)
        d_s = probs * (d_probs - delta)
        d_sb = d_s.astype(BF16)
        col["att_h"].append(att_h)
        col["dq_h"].append(dot(col["k_t"][rows], d_sb))
        dk_h = dot(d_sb, jnp.where(own, col["q"], zero))
        dv_h = dot(probs_b, jnp.where(own, col["d_att"], zero))
        col["d_k"] = dk_h if h == 0 else col["d_k"] + dk_h
        col["d_v"] = dv_h if h == 0 else col["d_v"] + dv_h
        return d_s

    def finish(col):
        att_t = jnp.concatenate(col["att_h"], axis=0)
        gate_t = col["gate_t"]
        mixed_t = (gate_t * att_t).astype(BF16)
        d_gate_t = (col["d_mixed_t"] * att_t * gate_t * (1.0 - gate_t)).astype(BF16)
        d_q_t = (jnp.concatenate(col["dq_h"], axis=0) * SCALE).astype(BF16)
        d_proj = jnp.concatenate(
            [d_q_t.T, (col["d_k"] * SCALE).astype(BF16), col["d_v"].astype(BF16), d_gate_t.T],
            axis=1,
        )
        d_tokens = dot(d_proj, wt_ref[...])
        return dot(col["tokens"], d_proj, 0, 0), dot(mixed_t, col["grads"]), d_tokens

    def bias_of(h):
        return (
            jnp.concatenate(
                [
                    jnp.concatenate([cols_ref[4 * h + 2 * r], cols_ref[4 * h + 2 * r + 1]], axis=1)
                    for r in range(2)
                ],
                axis=0,
            ).astype(F32)
            * LOG2E
        )

    cols = [prepare(t) for t in range(4)]
    order = [(h, t) for h in range(2) for t in range(4)]
    ahead = raw(cols[0], 0)
    for step, (h, t) in enumerate(order):
        s, d_probs = ahead
        if step + 1 < len(order):
            ahead = raw(cols[order[step + 1][1]], order[step + 1][0])
        if t == 0:
            bias, total = bias_of(h), 0.0
        total = total + head(cols[t], h, bias, s, d_probs)
        if t == 3:
            for r in range(2):
                for m in range(2):
                    part = member(total[r * 128 : (r + 1) * 128], m).astype(BF16)
                    for half in range(2):
                        out_ref[8 * h + 4 * m + 2 * r + half] = part[
                            :, half * 128 : (half + 1) * 128
                        ]
    d_w, d_wout = 0.0, 0.0
    for t in range(4):
        part_w, part_wout, d_tokens = finish(cols[t])
        d_w, d_wout = d_w + part_w, d_wout + part_wout
        for r in range(2):
            for m in range(2):
                at = 16 + 8 * m + 4 * (t // 2) + 2 * r + t % 2
                out_ref[at] = member(d_tokens[r * 128 : (r + 1) * 128], m).astype(BF16)
    d_w = d_w.astype(BF16)
    for u in range(2):
        for block in range(2):
            out_ref[32 + 2 * u + block] = d_w[
                u * 64 : (u + 1) * 64, block * C : (block + 1) * C
            ]
    out_ref[36] = d_wout.astype(BF16)
    out_ref[37] = jnp.zeros((64, C), BF16)


def vmem(count):
    return [pl.BlockSpec(memory_space=pltpu.VMEM)] * count


def attention(cols, grads, w, w_t, w_out):
    return pl.pallas_call(
        attention_kernel,
        out_shape=jax.ShapeDtypeStruct((38, 64, C), BF16),
        in_specs=vmem(5),
        out_specs=vmem(1)[0],
        compiler_params=pltpu.CompilerParams(vmem_limit_bytes=24 << 20),
        cost_estimate=pl.CostEstimate(
            flops=900_000_000, bytes_accessed=3_000_000, transcendentals=600_000
        ),
    )(cols, grads, w, w_t, w_out)


def middle_kernel(back_ref, xn_ref, normed_ref, wbias_ref, out_ref, d_xn_ref):
    def sums(row):
        return jnp.sum(back_ref[row].astype(F32), axis=0, keepdims=True)

    w_three = jnp.concatenate([wbias_ref[...]] * 3, axis=0).astype(BF16)
    d_wbias, d_gain = 0.0, 0.0
    for plane in range(8):
        m, cell = plane // 4, plane % 4
        owned = jnp.concatenate([sums(plane), sums(8 + plane)], axis=0)
        terms = [owned.astype(BF16)]
        left = owned - terms[0].astype(F32)
        terms.append(left.astype(BF16))
        terms.append((left - terms[1].astype(F32)).astype(BF16))
        three = jnp.concatenate(terms, axis=0)
        d_bias_x = dot(three, w_three, 0, 0)
        at = 16 + 8 * m + cell
        d_att_x = jnp.concatenate(
            [back_ref[at + 4 * j].astype(F32).reshape(8, 1, 8, C) for j in range(2)], axis=1
        )
        d_xn = d_att_x.reshape(128, C) + d_bias_x
        d_xn_ref[plane] = d_xn
        d_gain = d_gain + jnp.sum(d_xn * normed_ref[plane], axis=0, keepdims=True)
        parts = dot(three, xn_ref[plane])
        d_wbias = d_wbias + (parts[:2] + parts[2:4] + parts[4:])
    rows = jnp.concatenate([sums(row) for row in range(32, 37)] + [d_wbias, d_gain], axis=0)
    out_ref[...] = jnp.broadcast_to(rows[None], (DEV, 8, C)).astype(BF16)


def middle(back, xn, normed, heads_bias):
    return pl.pallas_call(
        middle_kernel,
        out_shape=(
            jax.ShapeDtypeStruct((DEV, 8, C), BF16),
            jax.ShapeDtypeStruct((8, DEV, C), F32),
        ),
        in_specs=vmem(4),
        out_specs=tuple(vmem(2)),
        compiler_params=pltpu.CompilerParams(vmem_limit_bytes=16 << 20),
    )(back, xn, normed, heads_bias)


def totals_kernel(planes_ref, w_ref, wout_ref, wbias_ref, gain_ref):
    scale = 1.0 / N

    def parts(row):
        plane = planes_ref[row].astype(F32) * scale
        return [member(plane, m) for m in range(2)]

    for u in range(2):
        for block in range(4):
            at = slice((block % 2) * W, (block % 2 + 1) * W)
            w_ref[u * 64 : (u + 1) * 64, block * C : (block + 1) * C] = jnp.concatenate(
                [part[:, at] for part in parts(2 * u + block // 2)], axis=1
            )
    for m, part in enumerate(parts(4)):
        wout_ref[m * W : (m + 1) * W] = part
    for h in range(2):
        for m, part in enumerate(parts(5 + h)):
            wbias_ref[2 * m + h : 2 * m + h + 1] = jnp.sum(part, axis=0, keepdims=True)
    gain_ref[...] = jnp.sum(planes_ref[7].astype(F32), axis=0, keepdims=True) * scale


def totals(planes):
    return pl.pallas_call(
        totals_kernel,
        out_shape=(
            jax.ShapeDtypeStruct((C, 4 * C), F32),
            jax.ShapeDtypeStruct((C, C), F32),
            jax.ShapeDtypeStruct((H, C), F32),
            jax.ShapeDtypeStruct((1, C), F32),
        ),
        in_specs=vmem(1),
        out_specs=tuple(vmem(4)),
        compiler_params=pltpu.CompilerParams(vmem_limit_bytes=8 << 20),
    )(planes)


def exchanged(blocks, axes=ROW):
    return lax.all_to_all(blocks, axes, split_axis=0, concat_axis=0, tiled=True)


def per_device(pair, out_grad, w_qkvg, w_out, w_bias, gain):
    sent = pack(pair, gain, w_bias)
    sent, pair, out_grad = lax.optimization_barrier((sent, pair, out_grad))
    mine = lax.axis_index("row_1")
    partner = [(0, 1), (1, 0)]
    cells = pair.reshape(2, 128, 2, C).transpose(0, 2, 1, 3).reshape(4, 128, C)
    grads = out_grad.reshape(128, 2, 2, C).transpose(2, 1, 0, 3).reshape(4, 128, C)
    both = jnp.concatenate([grads, cells], axis=0)
    other = lax.ppermute(both, "row_1", partner)
    first, second = jnp.where(mine == 0, both, other), jnp.where(mine == 0, other, both)
    grads = jnp.concatenate([first[:4], second[:4]], axis=0).reshape(4, N, C)
    xn, normed, inv_std = normalize(jnp.concatenate([first[4:], second[4:]], axis=0), gain)
    heads_bias = lax.dynamic_slice_in_dim(w_bias.T.astype(F32), 2 * mine, 2, axis=0)
    grads, xn, normed, inv_std, gain, heads_bias = lax.optimization_barrier(
        (grads, xn, normed, inv_std, gain, heads_bias)
    )
    w_own = lax.dynamic_index_in_dim(
        w_qkvg.reshape(C, 4, 2, W), mine, axis=2, keepdims=False
    ).reshape(C, 4 * W)
    wout_own = lax.dynamic_slice_in_dim(w_out, mine * W, W, axis=0)
    cols = exchanged(sent).transpose(1, 0, 2)
    planes = attention(cols, grads, w_own, w_own.T, wout_own)
    back = exchanged(planes.transpose(1, 0, 2).reshape(64, 19, 2, C), ("row_0", "row_2"))
    back = back.reshape(64, 38, C).transpose(1, 0, 2)
    last, d_xn = middle(back, xn, normed, heads_bias)
    last, d_xn = lax.optimization_barrier((last, d_xn))
    arrived = exchanged(last)
    moved = lax.ppermute(jnp.where(mine == 0, d_xn[4:], d_xn[:4]).astype(BF16), "row_1", partner)

    def own(planes):
        return jnp.where(mine == 0, planes[:4], planes[4:])

    d_xn, normed, inv_std = own(d_xn) + moved.astype(F32), own(normed), own(inv_std)
    scaled = d_xn * gain
    d_pair = (
        inv_std
        * (
            scaled
            - jnp.mean(scaled, axis=-1, keepdims=True)
            - normed * jnp.mean(scaled * normed, axis=-1, keepdims=True)
        )
    ).astype(BF16)
    d_pair = d_pair.reshape(2, 2, 128, C).transpose(0, 2, 1, 3).reshape(2, N, C)
    d_w, d_wout, d_wbias, d_gain = totals(arrived.transpose(1, 0, 2))
    return d_pair, d_w, d_wout, d_wbias.T, d_gain[0]


def solution(mesh):
    split = Mesh(
        mesh.devices.reshape(mesh.shape["crop"], 8, 2, 8), ("crop", "row_0", "row_1", "row_2")
    )
    placed = (P(CROP_ROW, None, None), P("crop", ROW, None), P(), P(), P(), P())
    return jax.shard_map(
        per_device,
        mesh=split,
        in_specs=placed,
        out_specs=(
            P(CROP_ROW, None, None),
            P("crop", None),
            P("crop", None),
            P("crop", None),
            P("crop"),
        ),
        check_vma=False,
    )
```

profile of v0, /device:TPU:8, one launch (start us, length us, event | category | flops | bytes accessed | tf_op | source)
XLA Modules:
  0.0 106.7 jit_solution(12834702397513311238)
XLA Ops:
  0.6 0.0 copy-start
  0.6 2.2 %shard_map.101 = bf16[128,16,128]{2,1,0:T(8,128)(2,1)} custom-call(bf16[2,256,128]{2,1,0:T(8,128)(2,1)} %pair_ref.1, f32[1,128]{1,0:T(1,128)} %bitcast.54, bf16[4,128]{1,0:T(4,128)(2,1)} %bitcast.55), custom_call_target="tpu_custom_call" | custom-call | tf_op jit(solution)/shard_map/pallas_call | solution.py:68
  2.8 0.0 copy-start.1
  2.8 20.0 %all-to-all-start = ((bf16[128,16,128]{2,1,0:T(8,128)(2,1)}), bf16[128,16,128]{2,1,0:T(8,128)(2,1)S(1)}, u32[]{:S(2)}, u32[]{:S(2)}) async-start(bf16[128,16,128]{2,1,0:T(8,128)(2,1)} %shard_map.101), calls=%async_computation | async-start | bytes 1048576 | tf_op jit(solution)/shard_map/all_to_all | solution.py:290
  22.8 0.0 copy-done.1
  22.8 0.0 copy-start.2
  22.8 0.9 copy-done.2
  23.7 0.0 copy-start.3
  23.8 0.0 copy-start.5
  23.8 5.0 %collective-permute-start = (bf16[8,128,128]{2,1,0:T(8,128)(2,1)S(1)}, bf16[8,128,128]{2,1,0:T(8,128)(2,1)S(1)}, u32[]{:S(2)}, u32[]{:S(2)}) collective-permute-start(bf16[8,128,128]{2,1,0:T(8,128)(2,1)S(1)} %pad_maximum_fusion), channel_id=1, source_target_pairs={{0,8},{8,0},{1,9},{9,1},{2,10},{10,2},{3,11},{11,3},{4,12},{12,4},... | collective-permute-start | bytes 786440 | tf_op jit(solution)/shard_map/ppermute | solution.py:301
  28.8 0.0 copy-done.5
  28.9 0.0 copy-done.3
  28.9 0.1 copy.28
  29.0 0.1 copy.29.w_ref
  29.2 0.0 copy-done
  29.2 9.6 %collective-permute-done = bf16[8,128,128]{2,1,0:T(8,128)(2,1)S(1)} collective-permute-done((bf16[8,128,128]{2,1,0:T(8,128)(2,1)S(1)}, bf16[8,128,128]{2,1,0:T(8,128)(2,1)S(1)}, u32[]{:S(2)}, u32[]{:S(2)}) %collective-permute-start) | collective-permute-done | bytes 262176 | tf_op jit(solution)/shard_map/ppermute | solution.py:301
  38.9 0.1 convert_reduce_fusion
  39.1 0.4 fusion.2
  39.5 0.0 copy-start.4
  39.5 0.7 copy-done.4
  40.1 0.3 fusion
  40.5 4.3 %all-to-all-done = bf16[128,16,128]{2,1,0:T(8,128)(2,1)S(1)} async-done(((bf16[128,16,128]{2,1,0:T(8,128)(2,1)}), bf16[128,16,128]{2,1,0:T(8,128)(2,1)S(1)}, u32[]{:S(2)}, u32[]{:S(2)}) %all-to-all-start) | async-done | bytes 524320 | tf_op jit(solution)/shard_map/all_to_all | solution.py:290
  44.7 0.1 copy.36
  44.9 3.3 %shard_map.102 = bf16[38,64,128]{2,1,0:T(8,128)(2,1)S(1)} custom-call(bf16[16,128,128]{2,1,0:T(8,128)(2,1)S(1)} %bitcast.41, bf16[4,256,128]{2,1,0:T(8,128)(2,1)S(1)} %bitcast.42, bf16[128,256]{1,0:T(8,128)(2,1)S(1)} %copy.29.w_ref, bf16[256,128]{1,0:T(8,128)(2,1)S(1)} %bitcast.44, bf16[64,128]{1,0:T(8,128)(2,1)S(1)} %constant_dynamic-slice_fusion.wout_ref), custom_call_target="tpu_custom_call" | custom-call | flops 900000000 | bytes 3000000 | tf_op jit(solution)/shard_map/pallas_call | solution.py:200
  48.2 0.6 copy.30
  48.8 27.8 %all_to_all.15 = bf16[64,19,2,128]{3,2,1,0:T(2,128)(2,1)S(1)} all-to-all(bf16[64,19,2,128]{3,2,1,0:T(2,128)(2,1)S(1)} %copy.30), channel_id=1, replica_groups=mesh['crop'=4,'row_0'=8,'row_1'=2,'row_2'=8] {'row_0','row_2'}, dimensions={0} | all-to-all | bytes 1245184 | tf_op jit(solution)/shard_map/all_to_all | solution.py:290
  76.6 0.1 copy.31
  76.7 1.1 %shard_map.103 = (bf16[128,8,128]{2,1,0:T(8,128)(2,1)}, f32[8,128,128]{2,1,0:T(8,128)S(1)}) custom-call(bf16[38,64,128]{2,1,0:T(8,128)(2,1)S(1)} %bitcast.38, bf16[8,128,128]{2,1,0:T(8,128)(2,1)S(1)} %get-tuple-element.25.xn_ref, f32[8,128,128]{2,1,0:T(8,128)S(1)} %get-tuple-element.26.normed_ref, f32[2,128]{1,0:T(2,128)S(1)} %constant_dynamic-slice_fusion.2.wbias_ref), custom_call_target="tpu_custom_call" | custom-call | tf_op jit(solution)/shard_map/pallas_call | solution.py:241
  77.8 3.5 %collective-permute-start.1 = (bf16[4,128,128]{2,1,0:T(8,128)(2,1)S(1)}, bf16[4,128,128]{2,1,0:T(8,128)(2,1)S(1)}, u32[]{:S(2)}, u32[]{:S(2)}) collective-permute-start(bf16[4,128,128]{2,1,0:T(8,128)(2,1)S(1)} %select_convert_fusion), channel_id=1, source_target_pairs={{0,8},{8,0},{1,9},{9,1},{2,10},{10,2},{3,11},{11,3},{4,12},{12,4},... | collective-permute-start | bytes 393224 | tf_op jit(solution)/shard_map/ppermute | solution.py:320
  81.4 8.6 %all-to-all-start.2 = ((bf16[128,8,128]{2,1,0:T(8,128)(2,1)}), bf16[128,8,128]{2,1,0:T(8,128)(2,1)S(1)}, u32[]{:S(2)}, u32[]{:S(2)}) async-start(bf16[128,8,128]{2,1,0:T(8,128)(2,1)} %get-tuple-element.30), calls=%async_computation.2 | async-start | bytes 524288 | tf_op jit(solution)/shard_map/all_to_all | solution.py:290
  90.0 0.0 collective-permute-done.1
  90.0 0.2 fusion.4
  90.3 0.3 multiply_convert_fusion.1
  90.6 0.8 copy.32
  91.4 14.5 %all-to-all-done.2 = bf16[128,8,128]{2,1,0:T(8,128)(2,1)S(1)} async-done(((bf16[128,8,128]{2,1,0:T(8,128)(2,1)}), bf16[128,8,128]{2,1,0:T(8,128)(2,1)S(1)}, u32[]{:S(2)}, u32[]{:S(2)}) %all-to-all-start.2) | async-done | bytes 262176 | tf_op jit(solution)/shard_map/all_to_all | solution.py:290
  105.9 0.8 shard_map.104
  (17 shorter events, 0.3 us)
Async XLA Ops:
  0.6 28.5 %copy-start = (bf16[128,128]{1,0:T(8,128)(2,1)S(1)}, bf16[128,128]{1,0:T(8,128)(2,1)}, u32[]{:S(2)}) copy-start(bf16[128,128]{1,0:T(8,128)(2,1)} %param.9) | copy-start | bytes 98308
  2.8 20.0 %copy-start.1 = (bf16[2,256,128]{2,1,0:T(8,128)(2,1)S(1)}, bf16[2,256,128]{2,1,0:T(8,128)(2,1)}, u32[]{:S(2)}) copy-start(bf16[2,256,128]{2,1,0:T(8,128)(2,1)} %pair_ref.1) | copy-start | bytes 393220
  2.8 41.9 %all-to-all-start = ((bf16[128,16,128]{2,1,0:T(8,128)(2,1)}), bf16[128,16,128]{2,1,0:T(8,128)(2,1)S(1)}, u32[]{:S(2)}, u32[]{:S(2)}) async-start(bf16[128,16,128]{2,1,0:T(8,128)(2,1)} %shard_map.101), calls=%async_computation | async-start | bytes 1048576 | tf_op jit(solution)/shard_map/all_to_all | solution.py:290
  22.8 0.9 copy-start.2
  23.7 5.1 %copy-start.3 = (bf16[128,512]{1,0:T(8,128)(2,1)S(1)}, bf16[128,512]{1,0:T(8,128)(2,1)}, u32[]{:S(2)}) copy-start(bf16[128,512]{1,0:T(8,128)(2,1)} %param.8) | copy-start | bytes 393220
  23.8 5.1 %copy-start.5 = (bf16[128,4]{0,1:T(4,128)(2,1)S(1)}, bf16[128,4]{0,1:T(4,128)(2,1)}, u32[]{:S(2)}) copy-start(bf16[128,4]{0,1:T(4,128)(2,1)} %param.10) | copy-start | bytes 3076
  23.8 15.0 %collective-permute-start = (bf16[8,128,128]{2,1,0:T(8,128)(2,1)S(1)}, bf16[8,128,128]{2,1,0:T(8,128)(2,1)S(1)}, u32[]{:S(2)}, u32[]{:S(2)}) collective-permute-start(bf16[8,128,128]{2,1,0:T(8,128)(2,1)S(1)} %pad_maximum_fusion), channel_id=1, source_target_pairs={{0,8},{8,0},{1,9},{9,1},{2,10},{10,2},{3,11},{11,3},{4,12},{12,4},... | collective-permute-start | bytes 786440 | tf_op jit(solution)/shard_map/ppermute | solution.py:301
  39.5 0.7 copy-start.4
  77.8 12.2 %collective-permute-start.1 = (bf16[4,128,128]{2,1,0:T(8,128)(2,1)S(1)}, bf16[4,128,128]{2,1,0:T(8,128)(2,1)S(1)}, u32[]{:S(2)}, u32[]{:S(2)}) collective-permute-start(bf16[4,128,128]{2,1,0:T(8,128)(2,1)S(1)} %select_convert_fusion), channel_id=1, source_target_pairs={{0,8},{8,0},{1,9},{9,1},{2,10},{10,2},{3,11},{11,3},{4,12},{12,4},... | collective-permute-start | bytes 393224 | tf_op jit(solution)/shard_map/ppermute | solution.py:320
  81.4 24.4 %all-to-all-start.2 = ((bf16[128,8,128]{2,1,0:T(8,128)(2,1)}), bf16[128,8,128]{2,1,0:T(8,128)(2,1)S(1)}, u32[]{:S(2)}, u32[]{:S(2)}) async-start(bf16[128,8,128]{2,1,0:T(8,128)(2,1)} %get-tuple-element.30), calls=%async_computation.2 | async-start | bytes 524288 | tf_op jit(solution)/shard_map/all_to_all | solution.py:290
where the time goes:
time: 107 us
  starting transfers between devices  37.1 us (35%)
  waiting for transfers between devices  28.4 us (27%)
  blocking collectives  27.8 us (26%)
  Pallas kernels  7.39 us (7%)
  local copies, waits for them, and re-layouts  3.63 us (3%)
  other arithmetic  1.5 us (1%)
    all_to_all x2, starting transfers between devices, exchanged(): return lax.all_to_all(blocks, axes, split_axis=0, concat_axis=0, tiled=True)  28.5 us
    all_to_all x1, blocking collectives, exchanged(): return lax.all_to_all(blocks, axes, split_axis=0, concat_axis=0, tiled=True)  27.8 us
    all_to_all x2, waiting for transfers between devices, exchanged(): return lax.all_to_all(blocks, axes, split_axis=0, concat_axis=0, tiled=True)  18.8 us
    ppermute x1, waiting for transfers between devices, per_device(): other = lax.ppermute(both, 'row_1', partner)  9.6 us
    ppermute x1, starting transfers between devices, per_device(): other = lax.ppermute(both, 'row_1', partner)  5.04 us
    ppermute x1, starting transfers between devices, per_device(): lax.ppermute(jnp.where(mine == 0, d_xn[4:], d_xn[:4]).astype(BF16), 'row_...  3.55 us
    pallas_call x1, Pallas kernels, attention(): pl.pallas_call(attention_kernel, out_shape=jax.ShapeDtypeStruct((38, 64,...  3.3 us
    pallas_call x1, Pallas kernels, pack(): pl.pallas_call(pack_kernel, out_shape=jax.ShapeDtypeStruct((DEV, 16, C),...  2.16 us
  transfers between devices with their start and end apart: 4, of which 3 were waited for; matrix products, arithmetic and copies ran while one was open for 2% of the time, Pallas kernels for 0%

commit v1 on v0

--- a/solution.py
+++ b/solution.py
@@ -209,14 +209,15 @@
     )(cols, grads, w, w_t, w_out)
 
 
-def middle_kernel(back_ref, xn_ref, normed_ref, wbias_ref, out_ref, d_xn_ref):
+def middle_kernel(back_ref, cells_ref, rows_ref, out_ref, d_xn_ref):
     def sums(row):
         return jnp.sum(back_ref[row].astype(F32), axis=0, keepdims=True)
 
-    w_three = jnp.concatenate([wbias_ref[...]] * 3, axis=0).astype(BF16)
+    w_three = jnp.concatenate([rows_ref[:2]] * 3, axis=0).astype(BF16)
     d_wbias, d_gain = 0.0, 0.0
     for plane in range(8):
         m, cell = plane // 4, plane % 4
+        xn, normed, _ = normalize(cells_ref[plane], rows_ref[2:3])
         owned = jnp.concatenate([sums(plane), sums(8 + plane)], axis=0)
         terms = [owned.astype(BF16)]
         left = owned - terms[0].astype(F32)
@@ -230,24 +231,24 @@
         )
         d_xn = d_att_x.reshape(128, C) + d_bias_x
         d_xn_ref[plane] = d_xn
-        d_gain = d_gain + jnp.sum(d_xn * normed_ref[plane], axis=0, keepdims=True)
-        parts = dot(three, xn_ref[plane])
+        d_gain = d_gain + jnp.sum(d_xn * normed, axis=0, keepdims=True)
+        parts = dot(three, xn)
         d_wbias = d_wbias + (parts[:2] + parts[2:4] + parts[4:])
     rows = jnp.concatenate([sums(row) for row in range(32, 37)] + [d_wbias, d_gain], axis=0)
     out_ref[...] = jnp.broadcast_to(rows[None], (DEV, 8, C)).astype(BF16)
 
 
-def middle(back, xn, normed, heads_bias):
+def middle(back, cells, rows):
     return pl.pallas_call(
         middle_kernel,
         out_shape=(
             jax.ShapeDtypeStruct((DEV, 8, C), BF16),
             jax.ShapeDtypeStruct((8, DEV, C), F32),
         ),
-        in_specs=vmem(4),
+        in_specs=vmem(3),
         out_specs=tuple(vmem(2)),
         compiler_params=pltpu.CompilerParams(vmem_limit_bytes=16 << 20),
-    )(back, xn, normed, heads_bias)
+    )(back, cells, rows)
 
 
 def totals_kernel(planes_ref, w_ref, wout_ref, wbias_ref, gain_ref):
@@ -297,15 +298,17 @@
     partner = [(0, 1), (1, 0)]
     cells = pair.reshape(2, 128, 2, C).transpose(0, 2, 1, 3).reshape(4, 128, C)
     grads = out_grad.reshape(128, 2, 2, C).transpose(2, 1, 0, 3).reshape(4, 128, C)
-    both = jnp.concatenate([grads, cells], axis=0)
-    other = lax.ppermute(both, "row_1", partner)
-    first, second = jnp.where(mine == 0, both, other), jnp.where(mine == 0, other, both)
-    grads = jnp.concatenate([first[:4], second[:4]], axis=0).reshape(4, N, C)
-    xn, normed, inv_std = normalize(jnp.concatenate([first[4:], second[4:]], axis=0), gain)
-    heads_bias = lax.dynamic_slice_in_dim(w_bias.T.astype(F32), 2 * mine, 2, axis=0)
-    grads, xn, normed, inv_std, gain, heads_bias = lax.optimization_barrier(
-        (grads, xn, normed, inv_std, gain, heads_bias)
-    )
+
+    def in_order(own, other):
+        first, second = jnp.where(mine == 0, own, other), jnp.where(mine == 0, other, own)
+        return jnp.concatenate([first, second], axis=0)
+
+    other = lax.ppermute(jnp.concatenate([grads, cells], axis=0), "row_1", partner)
+    grads = in_order(grads, other[:4]).reshape(4, N, C)
+    pair_cells = in_order(cells, other[4:])
+    rows = lax.dynamic_slice_in_dim(w_bias.T.astype(F32), 2 * mine, 2, axis=0)
+    rows = jnp.concatenate([rows, gain[None]], axis=0)
+    grads, pair_cells, rows = lax.optimization_barrier((grads, pair_cells, rows))
     w_own = lax.dynamic_index_in_dim(
         w_qkvg.reshape(C, 4, 2, W), mine, axis=2, keepdims=False
     ).reshape(C, 4 * W)
@@ -314,15 +317,14 @@
     planes = attention(cols, grads, w_own, w_own.T, wout_own)
     back = exchanged(planes.transpose(1, 0, 2).reshape(64, 19, 2, C), ("row_0", "row_2"))
     back = back.reshape(64, 38, C).transpose(1, 0, 2)
-    last, d_xn = middle(back, xn, normed, heads_bias)
+    last, d_xn = middle(back, pair_cells, rows)
     last, d_xn = lax.optimization_barrier((last, d_xn))
     arrived = exchanged(last)
     moved = lax.ppermute(jnp.where(mine == 0, d_xn[4:], d_xn[:4]).astype(BF16), "row_1", partner)
 
-    def own(planes):
-        return jnp.where(mine == 0, planes[:4], planes[4:])
-
-    d_xn, normed, inv_std = own(d_xn) + moved.astype(F32), own(normed), own(inv_std)
+    moved, cells = lax.optimization_barrier((moved, cells))
+    _, normed, inv_std = normalize(cells, gain)
+    d_xn = jnp.where(mine == 0, d_xn[:4], d_xn[4:]) + moved.astype(F32)
     scaled = d_xn * gain
     d_pair = (
         inv_std

time: 107 us -> 106 us (level)
  blocking collectives: 27.8 us -> 26.2 us
    all_to_all x1, blocking collectives: 27.8 us -> 26.2 us  [exchanged(): return lax.all_to_all(blocks, axes, split_axis=0, concat_axis=0, tiled=True)]
    ppermute x1, waiting for transfers between devices: 9.6 us -> 8.31 us  [per_device(): lax.ppermute(jnp.concatenate([grads, cells], axis=0), 'row_1', partner)]
where the time goes in v1:
time: 106 us
  starting transfers between devices  37.1 us (35%)
  waiting for transfers between devices  28 us (26%)
  blocking collectives  26.2 us (25%)
  Pallas kernels  7.8 us (7%)
  local copies, waits for them, and re-layouts  4.24 us (4%)
  other arithmetic  1.28 us (1%)
    all_to_all x2, starting transfers between devices, exchanged(): return lax.all_to_all(blocks, axes, split_axis=0, concat_axis=0, tiled=True)  28.6 us
    all_to_all x1, blocking collectives, exchanged(): return lax.all_to_all(blocks, axes, split_axis=0, concat_axis=0, tiled=True)  26.2 us
    all_to_all x2, waiting for transfers between devices, exchanged(): return lax.all_to_all(blocks, axes, split_axis=0, concat_axis=0, tiled=True)  19.7 us
    ppermute x1, waiting for transfers between devices, per_device(): lax.ppermute(jnp.concatenate([grads, cells], axis=0), 'row_1', partner)  8.31 us
    ppermute x1, starting transfers between devices, per_device(): lax.ppermute(jnp.concatenate([grads, cells], axis=0), 'row_1', partner)  5.04 us
    ppermute x1, starting transfers between devices, per_device(): lax.ppermute(jnp.where(mine == 0, d_xn[4:], d_xn[:4]).astype(BF16), 'row_...  3.53 us
    pallas_call x1, Pallas kernels, attention(): pl.pallas_call(attention_kernel, out_shape=jax.ShapeDtypeStruct((38, 64,...  3.3 us
    unnamed x13, local copies, waits for them, and re-layouts  2.32 us
  transfers between devices with their start and end apart: 4, of which 3 were waited for; matrix products, arithmetic and copies ran while one was open for 2% of the time, Pallas kernels for 0%

profile of v1, /device:TPU:8, one launch (start us, length us, event | category | flops | bytes accessed | tf_op | source)
XLA Modules:
  0.0 105.6 jit_solution(6044937478586780782)
XLA Ops:
  0.6 0.0 copy-start
  0.6 2.2 %shard_map.101 = bf16[128,16,128]{2,1,0:T(8,128)(2,1)} custom-call(bf16[2,256,128]{2,1,0:T(8,128)(2,1)} %pair_ref.1, f32[1,128]{1,0:T(1,128)} %bitcast.56, bf16[4,128]{1,0:T(4,128)(2,1)} %bitcast.58), custom_call_target="tpu_custom_call" | custom-call | tf_op jit(solution)/shard_map/pallas_call | solution.py:68
  2.8 0.0 copy-start.2
  2.8 20.0 %all-to-all-start = ((bf16[128,16,128]{2,1,0:T(8,128)(2,1)}), bf16[128,16,128]{2,1,0:T(8,128)(2,1)S(1)}, u32[]{:S(2)}, u32[]{:S(2)}) async-start(bf16[128,16,128]{2,1,0:T(8,128)(2,1)} %shard_map.101), calls=%async_computation | async-start | bytes 1048576 | tf_op jit(solution)/shard_map/all_to_all | solution.py:291
  22.8 0.0 copy-done.2
  22.8 0.0 copy-start.1
  22.8 0.9 copy-done.1
  23.7 0.0 copy-start.3
  23.8 5.0 %collective-permute-start = (bf16[8,128,128]{2,1,0:T(8,128)(2,1)S(1)}, bf16[8,128,128]{2,1,0:T(8,128)(2,1)S(1)}, u32[]{:S(2)}, u32[]{:S(2)}) collective-permute-start(bf16[8,128,128]{2,1,0:T(8,128)(2,1)S(1)} %pad_maximum_fusion), channel_id=1, source_target_pairs={{0,8},{8,0},{1,9},{9,1},{2,10},{10,2},{3,11},{11,3},{4,12},{12,4},... | collective-permute-start | bytes 786440 | tf_op jit(solution)/shard_map/ppermute | solution.py:306
  28.8 0.0 copy-done.3
  28.8 0.1 copy.28
  29.0 0.0 copy-start.5
  29.0 0.7 copy-done.5
  29.7 0.1 copy.29.w_ref
  29.8 0.0 copy-start.4
  29.8 0.6 copy-done.4
  30.4 0.0 copy-done
  30.5 8.3 %collective-permute-done = bf16[8,128,128]{2,1,0:T(8,128)(2,1)S(1)} collective-permute-done((bf16[8,128,128]{2,1,0:T(8,128)(2,1)S(1)}, bf16[8,128,128]{2,1,0:T(8,128)(2,1)S(1)}, u32[]{:S(2)}, u32[]{:S(2)}) %collective-permute-start) | collective-permute-done | bytes 262176 | tf_op jit(solution)/shard_map/ppermute | solution.py:306
  38.8 0.1 broadcast_select_fusion.1
  38.9 5.8 %all-to-all-done = bf16[128,16,128]{2,1,0:T(8,128)(2,1)S(1)} async-done(((bf16[128,16,128]{2,1,0:T(8,128)(2,1)}), bf16[128,16,128]{2,1,0:T(8,128)(2,1)S(1)}, u32[]{:S(2)}, u32[]{:S(2)}) %all-to-all-start) | async-done | bytes 524320 | tf_op jit(solution)/shard_map/all_to_all | solution.py:291
  44.7 0.1 copy.36
  44.9 3.3 %shard_map.102 = bf16[38,64,128]{2,1,0:T(8,128)(2,1)S(1)} custom-call(bf16[16,128,128]{2,1,0:T(8,128)(2,1)S(1)} %bitcast.41, bf16[4,256,128]{2,1,0:T(8,128)(2,1)S(1)} %bitcast.44, bf16[128,256]{1,0:T(8,128)(2,1)S(1)} %copy.29.w_ref, bf16[256,128]{1,0:T(8,128)(2,1)S(1)} %bitcast.43, bf16[64,128]{1,0:T(8,128)(2,1)S(1)} %constant_dynamic-slice_fusion.wout_ref), custom_call_target="tpu_custom_call" | custom-call | flops 900000000 | bytes 3000000 | tf_op jit(solution)/shard_map/pallas_call | solution.py:200
  48.2 0.6 copy.30
  48.8 26.2 %all_to_all.15 = bf16[64,19,2,128]{3,2,1,0:T(2,128)(2,1)S(1)} all-to-all(bf16[64,19,2,128]{3,2,1,0:T(2,128)(2,1)S(1)} %copy.30), channel_id=1, replica_groups=mesh['crop'=4,'row_0'=8,'row_1'=2,'row_2'=8] {'row_0','row_2'}, dimensions={0} | all-to-all | bytes 1245184 | tf_op jit(solution)/shard_map/all_to_all | solution.py:291
  75.0 0.1 copy.31
  75.2 1.5 %shard_map.103 = (bf16[128,8,128]{2,1,0:T(8,128)(2,1)}, f32[8,128,128]{2,1,0:T(8,128)S(1)}) custom-call(bf16[38,64,128]{2,1,0:T(8,128)(2,1)S(1)} %bitcast.38, bf16[8,128,128]{2,1,0:T(8,128)(2,1)S(1)} %get-tuple-element.23.cells_ref, f32[3,128]{1,0:T(4,128)S(1)} %pad_maximum_fusion.3.rows_ref), custom_call_target="tpu_custom_call" | custom-call | tf_op jit(solution)/shard_map/pallas_call | solution.py:242
  76.7 3.5 %collective-permute-start.1 = (bf16[4,128,128]{2,1,0:T(8,128)(2,1)S(1)}, bf16[4,128,128]{2,1,0:T(8,128)(2,1)S(1)}, u32[]{:S(2)}, u32[]{:S(2)}) collective-permute-start(bf16[4,128,128]{2,1,0:T(8,128)(2,1)S(1)} %select_convert_fusion), channel_id=1, source_target_pairs={{0,8},{8,0},{1,9},{9,1},{2,10},{10,2},{3,11},{11,3},{4,12},{12,4},... | collective-permute-start | bytes 393224 | tf_op jit(solution)/shard_map/ppermute | solution.py:323
  80.3 8.6 %all-to-all-start.2 = ((bf16[128,8,128]{2,1,0:T(8,128)(2,1)}), bf16[128,8,128]{2,1,0:T(8,128)(2,1)S(1)}, u32[]{:S(2)}, u32[]{:S(2)}) async-start(bf16[128,8,128]{2,1,0:T(8,128)(2,1)} %get-tuple-element.28), calls=%async_computation.2 | async-start | bytes 524288 | tf_op jit(solution)/shard_map/all_to_all | solution.py:291
  88.9 0.0 collective-permute-done.1
  88.9 0.1 convert_reduce_fusion
  89.0 0.2 fusion.8
  89.3 0.4 fusion.9
  89.7 0.3 fusion.7
  90.0 0.8 copy.32
  90.8 13.9 %all-to-all-done.2 = bf16[128,8,128]{2,1,0:T(8,128)(2,1)S(1)} async-done(((bf16[128,8,128]{2,1,0:T(8,128)(2,1)}), bf16[128,8,128]{2,1,0:T(8,128)(2,1)S(1)}, u32[]{:S(2)}, u32[]{:S(2)}) %all-to-all-start.2) | async-done | bytes 262176 | tf_op jit(solution)/shard_map/all_to_all | solution.py:291
  104.7 0.8 shard_map.104
  (15 shorter events, 0.2 us)
Async XLA Ops:
  0.6 29.8 %copy-start = (bf16[128,128]{1,0:T(8,128)(2,1)S(1)}, bf16[128,128]{1,0:T(8,128)(2,1)}, u32[]{:S(2)}) copy-start(bf16[128,128]{1,0:T(8,128)(2,1)} %param.9) | copy-start | bytes 98308
  2.8 20.0 %copy-start.2 = (bf16[256,2,128]{2,1,0:T(2,128)(2,1)S(1)}, bf16[256,2,128]{2,1,0:T(2,128)(2,1)}, u32[]{:S(2)}) copy-start(bf16[256,2,128]{2,1,0:T(2,128)(2,1)} %param.7) | copy-start | bytes 393220
  2.8 41.9 %all-to-all-start = ((bf16[128,16,128]{2,1,0:T(8,128)(2,1)}), bf16[128,16,128]{2,1,0:T(8,128)(2,1)S(1)}, u32[]{:S(2)}, u32[]{:S(2)}) async-start(bf16[128,16,128]{2,1,0:T(8,128)(2,1)} %shard_map.101), calls=%async_computation | async-start | bytes 1048576 | tf_op jit(solution)/shard_map/all_to_all | solution.py:291
  22.8 0.9 copy-start.1
  23.7 5.1 %copy-start.3 = (bf16[128,512]{1,0:T(8,128)(2,1)S(1)}, bf16[128,512]{1,0:T(8,128)(2,1)}, u32[]{:S(2)}) copy-start(bf16[128,512]{1,0:T(8,128)(2,1)} %param.8) | copy-start | bytes 393220
  23.8 15.0 %collective-permute-start = (bf16[8,128,128]{2,1,0:T(8,128)(2,1)S(1)}, bf16[8,128,128]{2,1,0:T(8,128)(2,1)S(1)}, u32[]{:S(2)}, u32[]{:S(2)}) collective-permute-start(bf16[8,128,128]{2,1,0:T(8,128)(2,1)S(1)} %pad_maximum_fusion), channel_id=1, source_target_pairs={{0,8},{8,0},{1,9},{9,1},{2,10},{10,2},{3,11},{11,3},{4,12},{12,4},... | collective-permute-start | bytes 786440 | tf_op jit(solution)/shard_map/ppermute | solution.py:306
  29.0 0.7 copy-start.5
  29.8 0.7 copy-start.4
  76.7 12.2 %collective-permute-start.1 = (bf16[4,128,128]{2,1,0:T(8,128)(2,1)S(1)}, bf16[4,128,128]{2,1,0:T(8,128)(2,1)S(1)}, u32[]{:S(2)}, u32[]{:S(2)}) collective-permute-start(bf16[4,128,128]{2,1,0:T(8,128)(2,1)S(1)} %select_convert_fusion), channel_id=1, source_target_pairs={{0,8},{8,0},{1,9},{9,1},{2,10},{10,2},{3,11},{11,3},{4,12},{12,4},... | collective-permute-start | bytes 393224 | tf_op jit(solution)/shard_map/ppermute | solution.py:323
  80.3 24.4 %all-to-all-start.2 = ((bf16[128,8,128]{2,1,0:T(8,128)(2,1)}), bf16[128,8,128]{2,1,0:T(8,128)(2,1)S(1)}, u32[]{:S(2)}, u32[]{:S(2)}) async-start(bf16[128,8,128]{2,1,0:T(8,128)(2,1)} %get-tuple-element.28), calls=%async_computation.2 | async-start | bytes 524288 | tf_op jit(solution)/shard_map/all_to_all | solution.py:291

commit v2 on v1

--- a/solution.py
+++ b/solution.py
@@ -158,11 +158,11 @@
 
     cols = [prepare(t) for t in range(4)]
     order = [(h, t) for h in range(2) for t in range(4)]
-    ahead = raw(cols[0], 0)
+    ahead = [raw(cols[t], h) for h, t in order[:2]]
     for step, (h, t) in enumerate(order):
-        s, d_probs = ahead
-        if step + 1 < len(order):
-            ahead = raw(cols[order[step + 1][1]], order[step + 1][0])
+        s, d_probs = ahead.pop(0)
+        if step + 2 < len(order):
+            ahead.append(raw(cols[order[step + 2][1]], order[step + 2][0]))
         if t == 0:
             bias, total = bias_of(h), 0.0
         total = total + head(cols[t], h, bias, s, d_probs)

time: 106 us -> 106 us (level)
  no operation moved by 1% of the time
where the time goes in v2:
time: 106 us; the launch traced here: 105 us
  starting transfers between devices  37.1 us (35%)
  waiting for transfers between devices  28 us (26%)
  blocking collectives  26.2 us (25%)
  Pallas kernels  7.58 us (7%)
  local copies, waits for them, and re-layouts  4.24 us (4%)
  other arithmetic  1.28 us (1%)
    all_to_all x2, starting transfers between devices, exchanged(): return lax.all_to_all(blocks, axes, split_axis=0, concat_axis=0, tiled=True)  28.6 us
    all_to_all x1, blocking collectives, exchanged(): return lax.all_to_all(blocks, axes, split_axis=0, concat_axis=0, tiled=True)  26.2 us
    all_to_all x2, waiting for transfers between devices, exchanged(): return lax.all_to_all(blocks, axes, split_axis=0, concat_axis=0, tiled=True)  19.7 us
    ppermute x1, waiting for transfers between devices, per_device(): lax.ppermute(jnp.concatenate([grads, cells], axis=0), 'row_1', partner)  8.31 us
    ppermute x1, starting transfers between devices, per_device(): lax.ppermute(jnp.concatenate([grads, cells], axis=0), 'row_1', partner)  5.04 us
    ppermute x1, starting transfers between devices, per_device(): lax.ppermute(jnp.where(mine == 0, d_xn[4:], d_xn[:4]).astype(BF16), 'row_...  3.53 us
    pallas_call x1, Pallas kernels, attention(): pl.pallas_call(attention_kernel, out_shape=jax.ShapeDtypeStruct((38, 64,...  3.08 us
    unnamed x13, local copies, waits for them, and re-layouts  2.32 us
  transfers between devices with their start and end apart: 4, of which 3 were waited for; matrix products, arithmetic and copies ran while one was open for 2% of the time, Pallas kernels for 0%

profile of v2, /device:TPU:8, one launch (start us, length us, event | category | flops | bytes accessed | tf_op | source)
XLA Modules:
  0.0 105.3 jit_solution(3455081493148892316)
XLA Ops:
  0.6 0.0 copy-start
  0.6 2.2 %shard_map.101 = bf16[128,16,128]{2,1,0:T(8,128)(2,1)} custom-call(bf16[2,256,128]{2,1,0:T(8,128)(2,1)} %pair_ref.1, f32[1,128]{1,0:T(1,128)} %bitcast.56, bf16[4,128]{1,0:T(4,128)(2,1)} %bitcast.58), custom_call_target="tpu_custom_call" | custom-call | tf_op jit(solution)/shard_map/pallas_call | solution.py:68
  2.8 0.0 copy-start.2
  2.8 20.0 %all-to-all-start = ((bf16[128,16,128]{2,1,0:T(8,128)(2,1)}), bf16[128,16,128]{2,1,0:T(8,128)(2,1)S(1)}, u32[]{:S(2)}, u32[]{:S(2)}) async-start(bf16[128,16,128]{2,1,0:T(8,128)(2,1)} %shard_map.101), calls=%async_computation | async-start | bytes 1048576 | tf_op jit(solution)/shard_map/all_to_all | solution.py:291
  22.8 0.0 copy-done.2
  22.8 0.0 copy-start.1
  22.8 0.9 copy-done.1
  23.7 0.0 copy-start.3
  23.8 5.0 %collective-permute-start = (bf16[8,128,128]{2,1,0:T(8,128)(2,1)S(1)}, bf16[8,128,128]{2,1,0:T(8,128)(2,1)S(1)}, u32[]{:S(2)}, u32[]{:S(2)}) collective-permute-start(bf16[8,128,128]{2,1,0:T(8,128)(2,1)S(1)} %pad_maximum_fusion), channel_id=1, source_target_pairs={{0,8},{8,0},{1,9},{9,1},{2,10},{10,2},{3,11},{11,3},{4,12},{12,4},... | collective-permute-start | bytes 786440 | tf_op jit(solution)/shard_map/ppermute | solution.py:306
  28.8 0.0 copy-done.3
  28.8 0.1 copy.28
  29.0 0.0 copy-start.5
  29.0 0.7 copy-done.5
  29.7 0.1 copy.29.w_ref
  29.8 0.0 copy-start.4
  29.8 0.6 copy-done.4
  30.4 0.0 copy-done
  30.5 8.3 %collective-permute-done = bf16[8,128,128]{2,1,0:T(8,128)(2,1)S(1)} collective-permute-done((bf16[8,128,128]{2,1,0:T(8,128)(2,1)S(1)}, bf16[8,128,128]{2,1,0:T(8,128)(2,1)S(1)}, u32[]{:S(2)}, u32[]{:S(2)}) %collective-permute-start) | collective-permute-done | bytes 262176 | tf_op jit(solution)/shard_map/ppermute | solution.py:306
  38.8 0.1 broadcast_select_fusion.1
  38.9 5.8 %all-to-all-done = bf16[128,16,128]{2,1,0:T(8,128)(2,1)S(1)} async-done(((bf16[128,16,128]{2,1,0:T(8,128)(2,1)}), bf16[128,16,128]{2,1,0:T(8,128)(2,1)S(1)}, u32[]{:S(2)}, u32[]{:S(2)}) %all-to-all-start) | async-done | bytes 524320 | tf_op jit(solution)/shard_map/all_to_all | solution.py:291
  44.7 0.1 copy.36
  44.9 3.1 %shard_map.102 = bf16[38,64,128]{2,1,0:T(8,128)(2,1)S(1)} custom-call(bf16[16,128,128]{2,1,0:T(8,128)(2,1)S(1)} %bitcast.41, bf16[4,256,128]{2,1,0:T(8,128)(2,1)S(1)} %bitcast.44, bf16[128,256]{1,0:T(8,128)(2,1)S(1)} %copy.29.w_ref, bf16[256,128]{1,0:T(8,128)(2,1)S(1)} %bitcast.43, bf16[64,128]{1,0:T(8,128)(2,1)S(1)} %constant_dynamic-slice_fusion.wout_ref), custom_call_target="tpu_custom_call" | custom-call | flops 900000000 | bytes 3000000 | tf_op jit(solution)/shard_map/pallas_call | solution.py:200
  48.0 0.6 copy.30
  48.6 26.2 %all_to_all.15 = bf16[64,19,2,128]{3,2,1,0:T(2,128)(2,1)S(1)} all-to-all(bf16[64,19,2,128]{3,2,1,0:T(2,128)(2,1)S(1)} %copy.30), channel_id=1, replica_groups=mesh['crop'=4,'row_0'=8,'row_1'=2,'row_2'=8] {'row_0','row_2'}, dimensions={0} | all-to-all | bytes 1245184 | tf_op jit(solution)/shard_map/all_to_all | solution.py:291
  74.8 0.1 copy.31
  75.0 1.5 %shard_map.103 = (bf16[128,8,128]{2,1,0:T(8,128)(2,1)}, f32[8,128,128]{2,1,0:T(8,128)S(1)}) custom-call(bf16[38,64,128]{2,1,0:T(8,128)(2,1)S(1)} %bitcast.38, bf16[8,128,128]{2,1,0:T(8,128)(2,1)S(1)} %get-tuple-element.23.cells_ref, f32[3,128]{1,0:T(4,128)S(1)} %pad_maximum_fusion.3.rows_ref), custom_call_target="tpu_custom_call" | custom-call | tf_op jit(solution)/shard_map/pallas_call | solution.py:242
  76.5 3.5 %collective-permute-start.1 = (bf16[4,128,128]{2,1,0:T(8,128)(2,1)S(1)}, bf16[4,128,128]{2,1,0:T(8,128)(2,1)S(1)}, u32[]{:S(2)}, u32[]{:S(2)}) collective-permute-start(bf16[4,128,128]{2,1,0:T(8,128)(2,1)S(1)} %select_convert_fusion), channel_id=1, source_target_pairs={{0,8},{8,0},{1,9},{9,1},{2,10},{10,2},{3,11},{11,3},{4,12},{12,4},... | collective-permute-start | bytes 393224 | tf_op jit(solution)/shard_map/ppermute | solution.py:323
  80.0 8.6 %all-to-all-start.2 = ((bf16[128,8,128]{2,1,0:T(8,128)(2,1)}), bf16[128,8,128]{2,1,0:T(8,128)(2,1)S(1)}, u32[]{:S(2)}, u32[]{:S(2)}) async-start(bf16[128,8,128]{2,1,0:T(8,128)(2,1)} %get-tuple-element.28), calls=%async_computation.2 | async-start | bytes 524288 | tf_op jit(solution)/shard_map/all_to_all | solution.py:291
  88.6 0.0 collective-permute-done.1
  88.7 0.1 convert_reduce_fusion
  88.8 0.2 fusion.8
  89.0 0.4 fusion.9
  89.4 0.3 fusion.7
  89.8 0.8 copy.32
  90.6 13.9 %all-to-all-done.2 = bf16[128,8,128]{2,1,0:T(8,128)(2,1)S(1)} async-done(((bf16[128,8,128]{2,1,0:T(8,128)(2,1)}), bf16[128,8,128]{2,1,0:T(8,128)(2,1)S(1)}, u32[]{:S(2)}, u32[]{:S(2)}) %all-to-all-start.2) | async-done | bytes 262176 | tf_op jit(solution)/shard_map/all_to_all | solution.py:291
  104.5 0.8 shard_map.104
  (15 shorter events, 0.2 us)
Async XLA Ops:
  0.6 29.8 %copy-start = (bf16[128,128]{1,0:T(8,128)(2,1)S(1)}, bf16[128,128]{1,0:T(8,128)(2,1)}, u32[]{:S(2)}) copy-start(bf16[128,128]{1,0:T(8,128)(2,1)} %param.9) | copy-start | bytes 98308
  2.8 20.0 %copy-start.2 = (bf16[256,2,128]{2,1,0:T(2,128)(2,1)S(1)}, bf16[256,2,128]{2,1,0:T(2,128)(2,1)}, u32[]{:S(2)}) copy-start(bf16[256,2,128]{2,1,0:T(2,128)(2,1)} %param.7) | copy-start | bytes 393220
  2.8 41.9 %all-to-all-start = ((bf16[128,16,128]{2,1,0:T(8,128)(2,1)}), bf16[128,16,128]{2,1,0:T(8,128)(2,1)S(1)}, u32[]{:S(2)}, u32[]{:S(2)}) async-start(bf16[128,16,128]{2,1,0:T(8,128)(2,1)} %shard_map.101), calls=%async_computation | async-start | bytes 1048576 | tf_op jit(solution)/shard_map/all_to_all | solution.py:291
  22.8 0.9 copy-start.1
  23.7 5.1 %copy-start.3 = (bf16[128,512]{1,0:T(8,128)(2,1)S(1)}, bf16[128,512]{1,0:T(8,128)(2,1)}, u32[]{:S(2)}) copy-start(bf16[128,512]{1,0:T(8,128)(2,1)} %param.8) | copy-start | bytes 393220
  23.8 15.0 %collective-permute-start = (bf16[8,128,128]{2,1,0:T(8,128)(2,1)S(1)}, bf16[8,128,128]{2,1,0:T(8,128)(2,1)S(1)}, u32[]{:S(2)}, u32[]{:S(2)}) collective-permute-start(bf16[8,128,128]{2,1,0:T(8,128)(2,1)S(1)} %pad_maximum_fusion), channel_id=1, source_target_pairs={{0,8},{8,0},{1,9},{9,1},{2,10},{10,2},{3,11},{11,3},{4,12},{12,4},... | collective-permute-start | bytes 786440 | tf_op jit(solution)/shard_map/ppermute | solution.py:306
  29.0 0.7 copy-start.5
  29.8 0.7 copy-start.4
  76.5 12.1 %collective-permute-start.1 = (bf16[4,128,128]{2,1,0:T(8,128)(2,1)S(1)}, bf16[4,128,128]{2,1,0:T(8,128)(2,1)S(1)}, u32[]{:S(2)}, u32[]{:S(2)}) collective-permute-start(bf16[4,128,128]{2,1,0:T(8,128)(2,1)S(1)} %select_convert_fusion), channel_id=1, source_target_pairs={{0,8},{8,0},{1,9},{9,1},{2,10},{10,2},{3,11},{11,3},{4,12},{12,4},... | collective-permute-start | bytes 393224 | tf_op jit(solution)/shard_map/ppermute | solution.py:323
  80.0 24.4 %all-to-all-start.2 = ((bf16[128,8,128]{2,1,0:T(8,128)(2,1)}), bf16[128,8,128]{2,1,0:T(8,128)(2,1)S(1)}, u32[]{:S(2)}, u32[]{:S(2)}) async-start(bf16[128,8,128]{2,1,0:T(8,128)(2,1)} %get-tuple-element.28), calls=%async_computation.2 | async-start | bytes 524288 | tf_op jit(solution)/shard_map/all_to_all | solution.py:291

commit v3 on v2

--- a/solution.py
+++ b/solution.py
@@ -158,11 +158,11 @@
 
     cols = [prepare(t) for t in range(4)]
     order = [(h, t) for h in range(2) for t in range(4)]
-    ahead = [raw(cols[t], h) for h, t in order[:2]]
+    ahead = [raw(cols[t], h) for h, t in order[:3]]
     for step, (h, t) in enumerate(order):
         s, d_probs = ahead.pop(0)
-        if step + 2 < len(order):
-            ahead.append(raw(cols[order[step + 2][1]], order[step + 2][0]))
+        if step + 3 < len(order):
+            ahead.append(raw(cols[order[step + 3][1]], order[step + 3][0]))
         if t == 0:
             bias, total = bias_of(h), 0.0
         total = total + head(cols[t], h, bias, s, d_probs)

time: 106 us -> 106 us (level)
  no operation moved by 1% of the time
where the time goes in v3:
time: 106 us; the launch traced here: 105 us
  starting transfers between devices  37.1 us (35%)
  waiting for transfers between devices  28 us (26%)
  blocking collectives  26.2 us (25%)
  Pallas kernels  7.47 us (7%)
  local copies, waits for them, and re-layouts  4.24 us (4%)
  other arithmetic  1.28 us (1%)
    all_to_all x2, starting transfers between devices, exchanged(): return lax.all_to_all(blocks, axes, split_axis=0, concat_axis=0, tiled=True)  28.6 us
    all_to_all x1, blocking collectives, exchanged(): return lax.all_to_all(blocks, axes, split_axis=0, concat_axis=0, tiled=True)  26.2 us
    all_to_all x2, waiting for transfers between devices, exchanged(): return lax.all_to_all(blocks, axes, split_axis=0, concat_axis=0, tiled=True)  19.7 us
    ppermute x1, waiting for transfers between devices, per_device(): lax.ppermute(jnp.concatenate([grads, cells], axis=0), 'row_1', partner)  8.31 us
    ppermute x1, starting transfers between devices, per_device(): lax.ppermute(jnp.concatenate([grads, cells], axis=0), 'row_1', partner)  5.04 us
    ppermute x1, starting transfers between devices, per_device(): lax.ppermute(jnp.where(mine == 0, d_xn[4:], d_xn[:4]).astype(BF16), 'row_...  3.53 us
    pallas_call x1, Pallas kernels, attention(): pl.pallas_call(attention_kernel, out_shape=jax.ShapeDtypeStruct((38, 64,...  2.97 us
    unnamed x13, local copies, waits for them, and re-layouts  2.32 us
  transfers between devices with their start and end apart: 4, of which 3 were waited for; matrix products, arithmetic and copies ran while one was open for 2% of the time, Pallas kernels for 0%

profile of v3, /device:TPU:8, one launch (start us, length us, event | category | flops | bytes accessed | tf_op | source)
XLA Modules:
  0.0 105.2 jit_solution(6956067895619245722)
XLA Ops:
  0.6 0.0 copy-start
  0.6 2.2 %shard_map.101 = bf16[128,16,128]{2,1,0:T(8,128)(2,1)} custom-call(bf16[2,256,128]{2,1,0:T(8,128)(2,1)} %pair_ref.1, f32[1,128]{1,0:T(1,128)} %bitcast.56, bf16[4,128]{1,0:T(4,128)(2,1)} %bitcast.58), custom_call_target="tpu_custom_call" | custom-call | tf_op jit(solution)/shard_map/pallas_call | solution.py:68
  2.8 0.0 copy-start.2
  2.8 20.0 %all-to-all-start = ((bf16[128,16,128]{2,1,0:T(8,128)(2,1)}), bf16[128,16,128]{2,1,0:T(8,128)(2,1)S(1)}, u32[]{:S(2)}, u32[]{:S(2)}) async-start(bf16[128,16,128]{2,1,0:T(8,128)(2,1)} %shard_map.101), calls=%async_computation | async-start | bytes 1048576 | tf_op jit(solution)/shard_map/all_to_all | solution.py:291
  22.8 0.0 copy-done.2
  22.8 0.0 copy-start.1
  22.8 0.9 copy-done.1
  23.7 0.0 copy-start.3
  23.8 5.0 %collective-permute-start = (bf16[8,128,128]{2,1,0:T(8,128)(2,1)S(1)}, bf16[8,128,128]{2,1,0:T(8,128)(2,1)S(1)}, u32[]{:S(2)}, u32[]{:S(2)}) collective-permute-start(bf16[8,128,128]{2,1,0:T(8,128)(2,1)S(1)} %pad_maximum_fusion), channel_id=1, source_target_pairs={{0,8},{8,0},{1,9},{9,1},{2,10},{10,2},{3,11},{11,3},{4,12},{12,4},... | collective-permute-start | bytes 786440 | tf_op jit(solution)/shard_map/ppermute | solution.py:306
  28.8 0.0 copy-done.3
  28.8 0.1 copy.28
  29.0 0.0 copy-start.5
  29.0 0.7 copy-done.5
  29.7 0.1 copy.29.w_ref
  29.8 0.0 copy-start.4
  29.8 0.6 copy-done.4
  30.4 0.0 copy-done
  30.5 8.3 %collective-permute-done = bf16[8,128,128]{2,1,0:T(8,128)(2,1)S(1)} collective-permute-done((bf16[8,128,128]{2,1,0:T(8,128)(2,1)S(1)}, bf16[8,128,128]{2,1,0:T(8,128)(2,1)S(1)}, u32[]{:S(2)}, u32[]{:S(2)}) %collective-permute-start) | collective-permute-done | bytes 262176 | tf_op jit(solution)/shard_map/ppermute | solution.py:306
  38.8 0.1 broadcast_select_fusion.1
  38.9 5.8 %all-to-all-done = bf16[128,16,128]{2,1,0:T(8,128)(2,1)S(1)} async-done(((bf16[128,16,128]{2,1,0:T(8,128)(2,1)}), bf16[128,16,128]{2,1,0:T(8,128)(2,1)S(1)}, u32[]{:S(2)}, u32[]{:S(2)}) %all-to-all-start) | async-done | bytes 524320 | tf_op jit(solution)/shard_map/all_to_all | solution.py:291
  44.7 0.1 copy.36
  44.9 3.0 %shard_map.102 = bf16[38,64,128]{2,1,0:T(8,128)(2,1)S(1)} custom-call(bf16[16,128,128]{2,1,0:T(8,128)(2,1)S(1)} %bitcast.41, bf16[4,256,128]{2,1,0:T(8,128)(2,1)S(1)} %bitcast.44, bf16[128,256]{1,0:T(8,128)(2,1)S(1)} %copy.29.w_ref, bf16[256,128]{1,0:T(8,128)(2,1)S(1)} %bitcast.43, bf16[64,128]{1,0:T(8,128)(2,1)S(1)} %constant_dynamic-slice_fusion.wout_ref), custom_call_target="tpu_custom_call" | custom-call | flops 900000000 | bytes 3000000 | tf_op jit(solution)/shard_map/pallas_call | solution.py:200
  47.8 0.6 copy.30
  48.5 26.2 %all_to_all.15 = bf16[64,19,2,128]{3,2,1,0:T(2,128)(2,1)S(1)} all-to-all(bf16[64,19,2,128]{3,2,1,0:T(2,128)(2,1)S(1)} %copy.30), channel_id=1, replica_groups=mesh['crop'=4,'row_0'=8,'row_1'=2,'row_2'=8] {'row_0','row_2'}, dimensions={0} | all-to-all | bytes 1245184 | tf_op jit(solution)/shard_map/all_to_all | solution.py:291
  74.7 0.1 copy.31
  74.9 1.5 %shard_map.103 = (bf16[128,8,128]{2,1,0:T(8,128)(2,1)}, f32[8,128,128]{2,1,0:T(8,128)S(1)}) custom-call(bf16[38,64,128]{2,1,0:T(8,128)(2,1)S(1)} %bitcast.38, bf16[8,128,128]{2,1,0:T(8,128)(2,1)S(1)} %get-tuple-element.23.cells_ref, f32[3,128]{1,0:T(4,128)S(1)} %pad_maximum_fusion.3.rows_ref), custom_call_target="tpu_custom_call" | custom-call | tf_op jit(solution)/shard_map/pallas_call | solution.py:242
  76.4 3.5 %collective-permute-start.1 = (bf16[4,128,128]{2,1,0:T(8,128)(2,1)S(1)}, bf16[4,128,128]{2,1,0:T(8,128)(2,1)S(1)}, u32[]{:S(2)}, u32[]{:S(2)}) collective-permute-start(bf16[4,128,128]{2,1,0:T(8,128)(2,1)S(1)} %select_convert_fusion), channel_id=1, source_target_pairs={{0,8},{8,0},{1,9},{9,1},{2,10},{10,2},{3,11},{11,3},{4,12},{12,4},... | collective-permute-start | bytes 393224 | tf_op jit(solution)/shard_map/ppermute | solution.py:323
  79.9 8.6 %all-to-all-start.2 = ((bf16[128,8,128]{2,1,0:T(8,128)(2,1)}), bf16[128,8,128]{2,1,0:T(8,128)(2,1)S(1)}, u32[]{:S(2)}, u32[]{:S(2)}) async-start(bf16[128,8,128]{2,1,0:T(8,128)(2,1)} %get-tuple-element.28), calls=%async_computation.2 | async-start | bytes 524288 | tf_op jit(solution)/shard_map/all_to_all | solution.py:291
  88.5 0.0 collective-permute-done.1
  88.5 0.1 convert_reduce_fusion
  88.7 0.2 fusion.8
  88.9 0.4 fusion.9
  89.3 0.3 fusion.7
  89.7 0.8 copy.32
  90.5 13.9 %all-to-all-done.2 = bf16[128,8,128]{2,1,0:T(8,128)(2,1)S(1)} async-done(((bf16[128,8,128]{2,1,0:T(8,128)(2,1)}), bf16[128,8,128]{2,1,0:T(8,128)(2,1)S(1)}, u32[]{:S(2)}, u32[]{:S(2)}) %all-to-all-start.2) | async-done | bytes 262176 | tf_op jit(solution)/shard_map/all_to_all | solution.py:291
  104.4 0.8 shard_map.104
  (15 shorter events, 0.2 us)
Async XLA Ops:
  0.6 29.8 %copy-start = (bf16[128,128]{1,0:T(8,128)(2,1)S(1)}, bf16[128,128]{1,0:T(8,128)(2,1)}, u32[]{:S(2)}) copy-start(bf16[128,128]{1,0:T(8,128)(2,1)} %param.9) | copy-start | bytes 98308
  2.8 20.0 %copy-start.2 = (bf16[256,2,128]{2,1,0:T(2,128)(2,1)S(1)}, bf16[256,2,128]{2,1,0:T(2,128)(2,1)}, u32[]{:S(2)}) copy-start(bf16[256,2,128]{2,1,0:T(2,128)(2,1)} %param.7) | copy-start | bytes 393220
  2.8 41.9 %all-to-all-start = ((bf16[128,16,128]{2,1,0:T(8,128)(2,1)}), bf16[128,16,128]{2,1,0:T(8,128)(2,1)S(1)}, u32[]{:S(2)}, u32[]{:S(2)}) async-start(bf16[128,16,128]{2,1,0:T(8,128)(2,1)} %shard_map.101), calls=%async_computation | async-start | bytes 1048576 | tf_op jit(solution)/shard_map/all_to_all | solution.py:291
  22.8 0.9 copy-start.1
  23.7 5.1 %copy-start.3 = (bf16[128,512]{1,0:T(8,128)(2,1)S(1)}, bf16[128,512]{1,0:T(8,128)(2,1)}, u32[]{:S(2)}) copy-start(bf16[128,512]{1,0:T(8,128)(2,1)} %param.8) | copy-start | bytes 393220
  23.8 15.0 %collective-permute-start = (bf16[8,128,128]{2,1,0:T(8,128)(2,1)S(1)}, bf16[8,128,128]{2,1,0:T(8,128)(2,1)S(1)}, u32[]{:S(2)}, u32[]{:S(2)}) collective-permute-start(bf16[8,128,128]{2,1,0:T(8,128)(2,1)S(1)} %pad_maximum_fusion), channel_id=1, source_target_pairs={{0,8},{8,0},{1,9},{9,1},{2,10},{10,2},{3,11},{11,3},{4,12},{12,4},... | collective-permute-start | bytes 786440 | tf_op jit(solution)/shard_map/ppermute | solution.py:306
  29.0 0.7 copy-start.5
  29.8 0.7 copy-start.4
  76.4 12.1 %collective-permute-start.1 = (bf16[4,128,128]{2,1,0:T(8,128)(2,1)S(1)}, bf16[4,128,128]{2,1,0:T(8,128)(2,1)S(1)}, u32[]{:S(2)}, u32[]{:S(2)}) collective-permute-start(bf16[4,128,128]{2,1,0:T(8,128)(2,1)S(1)} %select_convert_fusion), channel_id=1, source_target_pairs={{0,8},{8,0},{1,9},{9,1},{2,10},{10,2},{3,11},{11,3},{4,12},{12,4},... | collective-permute-start | bytes 393224 | tf_op jit(solution)/shard_map/ppermute | solution.py:323
  79.9 24.4 %all-to-all-start.2 = ((bf16[128,8,128]{2,1,0:T(8,128)(2,1)}), bf16[128,8,128]{2,1,0:T(8,128)(2,1)S(1)}, u32[]{:S(2)}, u32[]{:S(2)}) async-start(bf16[128,8,128]{2,1,0:T(8,128)(2,1)} %get-tuple-element.28), calls=%async_computation.2 | async-start | bytes 524288 | tf_op jit(solution)/shard_map/all_to_all | solution.py:291
